TPU v7x, 256 devices: a whole 4x4x8 slice. The times are simulated.
256 devices in a mesh: walker: 64 (over x_hi, y, z), freq: 4 (over x_lo, core).
Axes of the slice: x: 4 (x_hi: 2, x_lo: 2; x = x_hi * 2 + x_lo), y: 4, z: 8, core: 2. Of those that a mesh axis runs over, the one named last changes fastest.
Arguments:
- green_up_blocks: bfloat16 [64, 1, 4, 4288], P('walker', None, 'freq'), may hold values from -6 to 6
- green_down_blocks: bfloat16 [64, 1, 4, 4288], P('walker', None, 'freq'), may hold values from -6 to 6
- nu_index: int32 [4], P('freq'), may hold values from 0 to 3, each once
- q_index: int32 [4], P('freq'), may hold values from 0 to 63
- source: float32 [4, 4096], P('freq', 'walker'), may hold values from -6 to 6
Outputs:
- g4: float32 [4, 4096, 4096], P('freq', 'walker')
- response: float32 [4, 4096], P('freq', 'walker')
All inputs are finite; a program needn't handle non-finite values.
Results may differ from a plain program's by a relative error of at most 0.004.
Values may be sent and summed in bfloat16 or wider, within the bound.
No kernel may reach another device: no remote copies, remote signals or barrier semaphores. Data moves between devices by JAX's collectives and lax.ppermute only.
A program may use at most 64 MiB of HBM per device.

v0:
```python
import math
import jax
import jax.numpy as jnp
from jax import lax
from jax.sharding import PartitionSpec as P

SIDE = 8
CLUSTER_MOMENTUM = 64
W = 64
NU = 4
ITERS = 2


def cluster_sum(sites, shift):
    return (sites // SIDE + shift // SIDE) % SIDE * SIDE + (sites % SIDE + shift % SIDE) % SIDE


def products(block, sites, shift, offset):
    moved = cluster_sum(sites, shift)
    base = jnp.take(block, sites, axis=1)[:, :, :W].astype(jnp.float32)
    other = lax.dynamic_slice_in_dim(jnp.take(block, moved, axis=1), offset, W, 2).astype(
        jnp.float32
    )
    return (base * other).astype(jnp.bfloat16).reshape(block.shape[0], sites.shape[0] * W)


def stacked(block, sites, nu_index, q_index):
    return jnp.stack([products(block, sites, q_index[0], nu_index[0])])


def accumulate(left, right):
    return jnp.einsum("nrk,nrc->nkc", left, right, preferred_element_type=jnp.float32)


def shards(green_up_blocks, green_down_blocks, nu_index, q_index, source):
    up_all, down_all = (
        lax.all_gather(green_up_blocks, "freq", axis=2, tiled=True),
        lax.all_gather(green_down_blocks, "freq", axis=2, tiled=True),
    )
    extent = W + NU - 1
    rows_one = up_all.shape[1] * up_all.shape[2]
    walkers = lax.axis_size("walker")
    per_dev = CLUSTER_MOMENTUM // walkers
    owned = lax.axis_index("walker") * per_dev + jnp.arange(per_dev, dtype=jnp.int32)
    every = jnp.arange(CLUSTER_MOMENTUM, dtype=jnp.int32)

    def blocks(piece):
        return piece.reshape(-1, CLUSTER_MOMENTUM, extent)

    left = stacked(
        blocks(lax.all_gather(up_all, "walker", axis=0, tiled=True)), owned, nu_index, q_index
    )
    right = stacked(
        blocks(lax.all_gather(down_all, "walker", axis=0, tiled=True)), every, nu_index, q_index
    )
    summed = accumulate(left, right)
    kernel = summed * (1.0 / math.sqrt(walkers * rows_one))
    scale = 1.0 / (2.0 * math.sqrt(CLUSTER_MOMENTUM * W))
    start_vec = source.T
    current = start_vec
    for step in range(ITERS):

        def term(begin, sample_count, current=current):
            return jnp.einsum("kn,nkc->cn", current, kernel, precision=lax.Precision.HIGHEST)

        current = start_vec + scale * lax.psum_scatter(
            term(jnp.int32(0), lax.axis_size("walker") * (per_dev * W)),
            "walker",
            scatter_dimension=0,
            tiled=True,
        )
    return (kernel, current.T)


def solution(mesh):
    in_specs = (
        P("walker", None, "freq", None),
        P("walker", None, "freq", None),
        P("freq"),
        P("freq"),
        P("freq", "walker"),
    )
    out_specs = (P("freq", "walker", None), P("freq", "walker"))
    return jax.shard_map(shards, mesh=mesh, in_specs=in_specs, out_specs=out_specs, check_vma=False)
```

profile of v0, /device:TPU:2, one launch (start us, length us, event | category | flops | bytes accessed | tf_op | source)
XLA Modules:
  0.0 1031.1 jit_solution(13348956791322953057)
XLA Ops:
  7.2 0.0 all-gather.3.cloned.1.call-start
  7.2 5.7 all_gather.12
  13.0 0.6 copy.18
  13.6 0.0 all-gather.3.cloned.1.call-update
  13.6 0.0 all-gather.5.cloned.1.call-start
  13.6 5.7 all_gather.14
  19.4 0.6 copy.22
  20.0 0.0 all-gather.5.cloned.1.call-update
  20.0 0.0 reduce-scatter.7.cloned.1.call-start
  21.5 112.9 %all-gather.3.cloned.1.call-done = bf16[64,1,4,4288]{3,2,1,0:T(4,128)(2,1)} async-done(((bf16[1,1,4,4288]{3,2,1,0:T(4,128)(2,1)}), bf16[64,1,4,4288]{3,2,1,0:T(4,128)(2,1)}) %all-gather.3.cloned.1.call-update) | async-done | bytes 2195472 | tf_op jit(solution)/shard_map/all_gather | solution.py:51
  134.4 15.4 %reshape.59 = bf16[256,64,67]{2,1,0:T(8,128)(2,1)} reshape(bf16[64,1,4,4288]{3,2,1,0:T(4,128)(2,1)} %all-gather.3.cloned.1.call-done) | data formatting | bytes 4390912 | tf_op jit(solution)/shard_map/reshape | solution.py:48
  149.9 1.5 constant_dynamic-slice_fusion.1
  151.4 0.2 constant_dynamic-slice_fusion.2
  151.6 0.1 copy.32
  151.7 0.1 copy.31
  151.8 102.3 %all-gather.5.cloned.1.call-done = bf16[64,1,4,4288]{3,2,1,0:T(4,128)(2,1)} async-done(((bf16[1,1,4,4288]{3,2,1,0:T(4,128)(2,1)}), bf16[64,1,4,4288]{3,2,1,0:T(4,128)(2,1)}) %all-gather.5.cloned.1.call-update) | async-done | bytes 2195472 | tf_op jit(solution)/shard_map/all_gather | solution.py:54
  254.1 15.4 %reshape.61 = bf16[256,64,67]{2,1,0:T(8,128)(2,1)} reshape(bf16[64,1,4,4288]{3,2,1,0:T(4,128)(2,1)} %all-gather.5.cloned.1.call-done) | data formatting | bytes 4390912 | tf_op jit(solution)/shard_map/reshape | solution.py:48
  269.5 6.7 copy.23
  276.2 2.1 gather_fusion.1
  278.3 2.1 gather_fusion
  280.4 2.9 select_bitcast_fusion
  283.3 1.3 multiply_convert_fusion
  284.6 0.0 copy-start.1
  284.6 0.8 convolution_multiply_fusion
  285.3 0.0 copy-done.1
  285.3 0.0 copy-start
  285.3 4.8 convolution_bitcast_fusion.1
  290.1 0.0 reduce-scatter.7.cloned.1.call-update
  290.1 0.0 reduce-scatter.9.cloned.1.call-start
  290.2 365.8 %reduce-scatter.7.cloned.1.call-done = f32[64,1]{1,0:T(8,128)} async-done(((f32[4096,1]{1,0:T(8,128)}), f32[64,1]{1,0:T(8,128)}) %reduce-scatter.7.cloned.1.call-update) | async-done | bytes 272
  656.0 0.8 copy.26
  656.9 0.0 copy-done
  656.9 4.8 convolution_bitcast_fusion
  661.6 0.0 reduce-scatter.9.cloned.1.call-update
  661.7 361.6 %reduce-scatter.9.cloned.1.call-done = f32[64,1]{1,0:T(8,128)} async-done(((f32[4096,1]{1,0:T(8,128)}), f32[64,1]{1,0:T(8,128)}) %reduce-scatter.9.cloned.1.call-update) | async-done | bytes 272
  1023.2 0.8 copy.28
  1024.1 0.5 fusion.14
  (5 shorter events, 0.0 us)
Async XLA Ops:
  7.2 127.3 %all-gather.3.cloned.1.call-start = ((), (), s32[]{:S(2)}) async-start(), calls=%async_computation.2 | async-start | bytes 2263040 | tf_op jit(solution)/shard_map/all_gather | solution.py:51
  13.6 240.5 %all-gather.5.cloned.1.call-start = ((), (), s32[]{:S(2)}) async-start(), calls=%async_computation.3 | async-start | bytes 2263040 | tf_op jit(solution)/shard_map/all_gather | solution.py:54
  20.0 636.0 %reduce-scatter.7.cloned.1.call-start = ((), (), s32[]{:S(2)}) async-start(), calls=%async_computation.4 | async-start | bytes 2129920
  284.6 0.8 copy-start.1
  285.3 371.5 %copy-start = (f32[64,4096]{1,0:T(8,128)}, f32[64,4096]{1,0:T(8,128)S(1)}, u32[]{:S(2)}) copy-start(f32[64,4096]{1,0:T(8,128)S(1)} %convolution_multiply_fusion) | copy-start | bytes 3145732
  290.1 733.1 %reduce-scatter.9.cloned.1.call-start = ((), (), s32[]{:S(2)}) async-start(), calls=%async_computation.5 | async-start | bytes 2129920
Sparse Core Ops, SparseCore 0:
  13.7 120.6 all-gather.2
  138.6 115.4 all-gather.4
  290.3 365.7 reduce-scatter.6
  661.8 361.4 reduce-scatter.8
where the time goes:
time: 1030 us
  waiting for transfers between devices  943 us (92%)
  local copies, waits for them, and re-layouts  46.5 us (5%)
  between operations  15.3 us (1%)
  blocking collectives  11.5 us (1%)
  matrix products  10.3 us (1%)
    unnamed x6, waiting for transfers between devices  727 us
    all_gather x1, waiting for transfers between devices, shards(): lax.all_gather(up_all, 'walker', axis=0, tiled=True)  113 us
    all_gather x1, waiting for transfers between devices, shards(): lax.all_gather(down_all, 'walker', axis=0, tiled=True)  102 us
    reshape x3, local copies, waits for them, and re-layouts, blocks(): return piece.reshape(-1, CLUSTER_MOMENTUM, extent)  37.5 us
  transfers between devices with their start and end apart: 4, of which 4 were waited for; matrix products, arithmetic and copies ran while one was open for 2% of the time, Pallas kernels for 0%

commit v1 on v0

--- a/solution.py
+++ b/solution.py
@@ -51,7 +51,15 @@
         blocks(lax.all_gather(up_all, "walker", axis=0, tiled=True)), owned, nu_index, q_index
     )
     right = stacked(
-        blocks(lax.all_gather(down_all, "walker", axis=0, tiled=True)), every, nu_index, q_index
+        blocks(
+            jnp.concatenate(
+                lax.all_to_all(jnp.stack([down_all] * lax.axis_size("walker")), "walker", 0, 0),
+                axis=0,
+            )
+        ),
+        every,
+        nu_index,
+        q_index,
     )
     summed = accumulate(left, right)
     kernel = summed * (1.0 / math.sqrt(walkers * rows_one))

time: 1030 us -> 923 us (0.90)
  waiting for transfers between devices: 943 us -> 818 us
  starting transfers between devices: 0.16 us -> 14 us
    all_gather x1 -> x0, waiting for transfers between devices: 102 us -> none  [shards(): lax.all_gather(down_all, 'walker', axis=0, tiled=True)]
    all_gather x1, waiting for transfers between devices: 113 us -> 44.5 us  [shards(): lax.all_gather(up_all, 'walker', axis=0, tiled=True)]
    all_to_all x0 -> x1, waiting for transfers between devices: none -> 46 us  [shards(): lax.all_to_all(jnp.stack([down_all] * lax.axis_size('walker')), 'walker',...]
    another operation x0 -> x3, local copies, waits for them, and re-layouts: none -> 23.2 us  [the longest x2 21.3 us: blocks(): return piece.reshape(-1, CLUSTER_MOMENTUM, extent)]
    reshape x3 -> x1, local copies, waits for them, and re-layouts: 37.5 us -> 15.4 us  [blocks(): return piece.reshape(-1, CLUSTER_MOMENTUM, extent)]
    all_to_all x0 -> x1, starting transfers between devices: none -> 13.5 us  [shards(): lax.all_to_all(jnp.stack([down_all] * lax.axis_size('walker')), 'walker',...]
    unnamed x6 -> x5, waiting for transfers between devices: 727 us -> 727 us
  transfers between devices with their start and end apart: 4 -> 4, of which waited for: 4 -> 4; matrix products, arithmetic and copies ran while one was open for 2% -> 3% of each run, Pallas kernels for 0% -> 0%
where the time goes in v1:
time: 923 us
  waiting for transfers between devices  818 us (89%)
  local copies, waits for them, and re-layouts  47.1 us (5%)
  between operations  15.3 us (2%)
  starting transfers between devices  14 us (2%)
  blocking collectives  13.4 us (1%)
  matrix products  10.3 us (1%)
    unnamed x5, waiting for transfers between devices  727 us
    all_to_all x1, waiting for transfers between devices, shards(): lax.all_to_all(jnp.stack([down_all] * lax.axis_size('walker')), 'walker',...  46 us
    all_gather x1, waiting for transfers between devices, shards(): lax.all_gather(up_all, 'walker', axis=0, tiled=True)  44.5 us
    another operation x2, local copies, waits for them, and re-layouts, blocks(): return piece.reshape(-1, CLUSTER_MOMENTUM, extent)  21.3 us
  transfers between devices with their start and end apart: 4, of which 4 were waited for; matrix products, arithmetic and copies ran while one was open for 3% of the time, Pallas kernels for 0%

profile of v1, /device:TPU:2, one launch (start us, length us, event | category | flops | bytes accessed | tf_op | source)
XLA Modules:
  0.0 922.6 jit_solution(3342087112266298839)
XLA Ops:
  7.2 5.7 all_gather.13
  12.9 2.0 stack.2
  14.9 0.0 copy-start.1
  14.9 13.5 %all-to-all-start = ((bf16[64,1,1,4,4288]{4,3,2,1,0:T(4,128)(2,1)}), bf16[64,1,1,4,4288]{4,3,2,1,0:T(4,128)(2,1)S(1)}, u32[]{:S(2)}, u32[]{:S(2)}) async-start(bf16[64,1,1,4,4288]{4,3,2,1,0:T(4,128)(2,1)} %stack.2), calls=%async_computation | async-start | bytes 4456448 | tf_op jit(solution)/shard_map/all_to_all | solution.py:56
  28.4 0.0 all-gather.2.cloned.1.call-start
  28.5 0.0 copy-done.1
  28.5 7.7 all_gather.11
  36.2 0.6 copy.23
  36.8 0.0 all-gather.2.cloned.1.call-update
  36.8 0.2 reduce-scatter.7.cloned.1.call-start
  38.5 46.0 %all-to-all-done = bf16[64,1,1,4,4288]{4,3,2,1,0:T(4,128)(2,1)S(1)} async-done(((bf16[64,1,1,4,4288]{4,3,2,1,0:T(4,128)(2,1)}), bf16[64,1,1,4,4288]{4,3,2,1,0:T(4,128)(2,1)S(1)}, u32[]{:S(2)}, u32[]{:S(2)}) %all-to-all-start) | async-done | bytes 2195488 | tf_op jit(solution)/shard_map/all_to_all | solution.py:56
  84.6 14.8 %reshape_reshape.3 = bf16[256,64,67]{2,1,0:T(8,128)(2,1)} reshape(bf16[64,1,1,4,4288]{4,3,2,1,0:T(4,128)(2,1)S(1)} %all-to-all-done) | data formatting | bytes 4390912 | tf_op jit(solution)/shard_map/reshape;reshape | solution.py:48
  99.3 6.5 copy.27
  105.9 2.1 gather_fusion.1
  108.0 2.1 gather_fusion
  110.1 2.9 select_bitcast_fusion
  113.0 1.3 multiply_convert_fusion
  114.2 44.5 %all-gather.2.cloned.1.call-done = bf16[64,1,4,4288]{3,2,1,0:T(4,128)(2,1)} async-done(((bf16[1,1,4,4288]{3,2,1,0:T(4,128)(2,1)}), bf16[64,1,4,4288]{3,2,1,0:T(4,128)(2,1)}) %all-gather.2.cloned.1.call-update) | async-done | bytes 2195472 | tf_op jit(solution)/shard_map/all_gather | solution.py:51
  158.8 15.4 %reshape.59 = bf16[256,64,67]{2,1,0:T(8,128)(2,1)} reshape(bf16[64,1,4,4288]{3,2,1,0:T(4,128)(2,1)} %all-gather.2.cloned.1.call-done) | data formatting | bytes 4390912 | tf_op jit(solution)/shard_map/reshape | solution.py:48
  174.2 0.0 copy-start.2
  174.2 1.5 constant_dynamic-slice_fusion.1
  175.7 0.2 constant_dynamic-slice_fusion.2
  175.9 0.1 copy.37
  176.0 0.1 copy.36
  176.1 0.8 convolution_multiply_fusion
  176.9 0.0 copy-done.2
  176.9 0.0 copy-start
  176.9 4.8 convolution_bitcast_fusion.1
  181.7 0.0 reduce-scatter.7.cloned.1.call-update
  181.7 0.3 reduce-scatter.9.cloned.1.call-start
  182.0 365.7 %reduce-scatter.7.cloned.1.call-done = f32[64,1]{1,0:T(8,128)} async-done(((f32[4096,1]{1,0:T(8,128)}), f32[64,1]{1,0:T(8,128)}) %reduce-scatter.7.cloned.1.call-update) | async-done | bytes 272
  547.7 0.8 copy.30
  548.5 0.0 copy-done
  548.5 4.8 convolution_bitcast_fusion
  553.3 0.0 reduce-scatter.9.cloned.1.call-update
  553.3 361.5 %reduce-scatter.9.cloned.1.call-done = f32[64,1]{1,0:T(8,128)} async-done(((f32[4096,1]{1,0:T(8,128)}), f32[64,1]{1,0:T(8,128)}) %reduce-scatter.9.cloned.1.call-update) | async-done | bytes 272
  914.8 0.8 copy.32
  915.6 0.5 fusion.14
  (6 shorter events, 0.1 us)
Async XLA Ops:
  14.9 13.6 %copy-start.1 = (bf16[1,1,1,4288]{3,2,1,0:T(2,128)(2,1)S(1)}, bf16[1,1,1,4288]{3,2,1,0:T(2,128)(2,1)}, u32[]{:S(2)}) copy-start(bf16[1,1,1,4288]{3,2,1,0:T(2,128)(2,1)} %param.9) | copy-start | bytes 25732
  14.9 69.7 %all-to-all-start = ((bf16[64,1,1,4,4288]{4,3,2,1,0:T(4,128)(2,1)}), bf16[64,1,1,4,4288]{4,3,2,1,0:T(4,128)(2,1)S(1)}, u32[]{:S(2)}, u32[]{:S(2)}) async-start(bf16[64,1,1,4,4288]{4,3,2,1,0:T(4,128)(2,1)} %stack.2), calls=%async_computation | async-start | bytes 4456448 | tf_op jit(solution)/shard_map/all_to_all | solution.py:56
  28.4 130.4 %all-gather.2.cloned.1.call-start = ((), (), s32[]{:S(2)}) async-start(), calls=%async_computation.3 | async-start | bytes 2263040 | tf_op jit(solution)/shard_map/all_gather | solution.py:51
  36.8 510.8 %reduce-scatter.7.cloned.1.call-start = ((), (), s32[]{:S(2)}) async-start(), calls=%async_computation.4 | async-start | bytes 2129920
  174.2 2.7 copy-start.2
  176.9 371.6 %copy-start = (f32[64,4096]{1,0:T(8,128)}, f32[64,4096]{1,0:T(8,128)S(1)}, u32[]{:S(2)}) copy-start(f32[64,4096]{1,0:T(8,128)S(1)} %convolution_multiply_fusion) | copy-start | bytes 3145732
  181.7 733.1 %reduce-scatter.9.cloned.1.call-start = ((), (), s32[]{:S(2)}) async-start(), calls=%async_computation.5 | async-start | bytes 2129920
Sparse Core Ops, SparseCore 0:
  37.0 121.7 all-gather.1
  181.8 365.8 reduce-scatter.6
  553.4 361.2 reduce-scatter.8
